TPU v7x, 1024 devices: a whole 4x8x16 slice. The times are simulated.
1024 devices in a mesh: context: 128 (over z_lo, y, core), tensor: 8 (over z_hi, x).
Axes of the slice: x: 4, y: 8, z: 16 (z_hi: 2, z_lo: 8; z = z_hi * 8 + z_lo), core: 2. Of those that a mesh axis runs over, the one named last changes fastest.
Arguments:
- query_proj: bfloat16 [16384, 4096], P('context', 'tensor'), may hold values from -6 to 6
- key_proj: bfloat16 [16384, 4096], P('context', 'tensor'), may hold values from -6 to 6
- value_proj: bfloat16 [16384, 4096], P('context', 'tensor'), may hold values from -6 to 6
- short_taps: float32 [3, 7, 4096], P(None, None, 'tensor'), may hold values from -2.4 to 2.4
- long_filter: float32 [8, 512, 16384], P('tensor', 'context'), may hold values from -1 to 1
- grad_mixed: bfloat16 [16384, 4096], P('context', 'tensor'), may hold values from -6 to 6
Outputs:
- mixed_out: bfloat16 [16384, 4096], P('context', 'tensor')
- input_grads: bfloat16 [3, 16384, 4096], P(None, 'context', 'tensor')
- filter_grad: float32 [8, 512, 16384], P('tensor', 'context')
All inputs are finite; a program needn't handle non-finite values.
Results may differ from a plain program's by a relative error of at most 0.0064.
Values may be sent and summed in bfloat16 or wider, within the bound.
A program may use at most 32 MiB of HBM per device.

v0:
```python
import math

import jax
import jax.numpy as jnp
import numpy as np
from jax import lax
from jax.experimental import pallas as pl
from jax.experimental.pallas import tpu as pltpu
from jax.sharding import PartitionSpec as P

MESH = pl.DeviceIdType.MESH
F32 = jnp.float32
BF16 = jnp.bfloat16
B = 128
SEQ = B * B
PER = 4
TAPS = 7


def split_np(table):
    high = table.astype(jnp.bfloat16)
    low = (table - high.astype(np.float64)).astype(jnp.bfloat16)
    return high, low


def build_tables():
    idx = np.arange(B)
    psi = 2.0 * np.pi * idx[:, None] * (idx[None, :] + 0.25) / B
    phi = 2.0 * np.pi * (idx[:, None] + 0.25) * idx[None, :] / SEQ
    two = 2.0 * np.pi * ((idx[:, None] * idx[None, :]) % B) / B
    first = np.concatenate([np.cos(psi).T, -np.sin(psi).T], axis=0)
    first_back = np.concatenate([np.cos(psi), -np.sin(psi)], axis=1)
    cos, sin = np.cos(two), np.sin(two)
    second = np.block([[cos, -sin], [sin, cos]])
    second_back = np.block([[cos, sin], [-sin, cos]])
    first_cat = np.concatenate(split_np(first), axis=1)
    back_cat = np.concatenate(split_np(first_back), axis=0)
    perm = np.zeros((2 * B, 2 * B))
    for s in range(B // PER):
        for j in range(PER):
            perm[s * 2 * PER + j, PER * s + j] = 1.0
            perm[s * 2 * PER + PER + j, B + PER * s + j] = 1.0
    squares = np.stack(
        [first_cat, *split_np(second), *split_np(second_back), back_cat, perm.astype(jnp.bfloat16)]
    )
    twist = np.stack([np.cos(phi), -np.sin(phi)]).astype(np.float32)
    return squares, twist


SQUARES, TWIST = build_tables()


def split(value):
    high = value.astype(BF16)
    return high, (value - high.astype(F32)).astype(BF16)


def dot(a, b):
    return jnp.dot(a, b, preferred_element_type=F32)


def kernel(
    q_in, k_in, v_in, g_in, taps_in, filt_in, squares_in, twist_in,
    mixed_out, grads_out, fgrad_out,
    q_v, k_v, v_v, g_v, taps, filt, squares, twist,
    ext, ext_back, conv, halo_s, halo_r, halo2_s, halo2_r,
    pair, send1, recv1, send2, recv2, x32, y32,
    mid_hi, mid_lo, spec, prod_hi, prod_lo,
    in_sems, dma_sems,
):
    me = lax.axis_index("context")
    n = B

    loads = [
        pltpu.make_async_copy(src, dst, in_sems.at[i])
        for i, (src, dst) in enumerate(
            [
                (q_in, q_v), (k_in, k_v), (v_in, v_v), (taps_in, taps),
                (g_in, g_v), (filt_in, filt), (squares_in, squares), (twist_in, twist),
            ]
        )
    ]
    for load in loads:
        load.start()

    barrier = pltpu.get_barrier_semaphore()

    @pl.loop(1, n)
    def _(i):
        pl.semaphore_signal(
            barrier, inc=1, device_id={"context": lax.rem(me + i, n)}, device_id_type=MESH
        )

    def exchange(src, dst, send_sem, recv_sem):
        @pl.loop(1, n)
        def _(i):
            peer = lax.rem(me + i, n)
            pltpu.make_async_remote_copy(
                src_ref=src.at[peer], dst_ref=dst.at[me], send_sem=send_sem, recv_sem=recv_sem,
                device_id={"context": peer}, device_id_type=MESH,
            ).start()

        dst[pl.ds(me, 1)] = src[pl.ds(me, 1)]

    def all_of(src, dst, send_sem, recv_sem):
        return pltpu.make_async_remote_copy(
            src_ref=src.at[pl.ds(0, n - 1)], dst_ref=dst.at[pl.ds(0, n - 1)],
            send_sem=send_sem, recv_sem=recv_sem,
            device_id={"context": lax.rem(me + 1, n)}, device_id_type=MESH,
        )

    def halo_copy(src, dst, send_sem, recv_sem, step):
        return pltpu.make_async_remote_copy(
            src_ref=src, dst_ref=dst, send_sem=send_sem, recv_sem=recv_sem,
            device_id={"context": lax.rem(me + step + n, n)}, device_id_type=MESH,
        )

    for load in loads[:4]:
        load.wait()
    for a, src in enumerate((q_v, k_v, v_v)):
        ext[a, 0:8, :] = jnp.zeros((8, ext.shape[2]), F32)
        halo_s[a] = src[B - 16 : B, :][8:16]

    loads[4].wait()

    def short(a, first_row, rows, cols):
        acc = taps[a, 0:1, cols] * ext[a, 8 + first_row : 8 + first_row + rows, cols]
        for j in range(1, TAPS):
            start = 8 + first_row - j
            acc = acc + taps[a, j : j + 1, cols] * ext[a, start : start + rows, cols]
        return acc

    def gate(first_row, rows, tile):
        cols = pl.ds(pl.multiple_of(tile * B, B), B)
        out = []
        for a in range(3):
            value = short(a, first_row, rows, cols)
            conv[a, first_row : first_row + rows, cols] = value
            out.append(value)
        here = slice(first_row, first_row + rows)
        wide = pl.multiple_of(tile * 2 * B, 2 * B)
        pair[here, pl.ds(wide, B)] = (out[1] * out[2]).astype(BF16)
        pair[here, pl.ds(wide + B, B)] = (g_v[here, cols].astype(F32) * out[0]).astype(BF16)

    @pl.loop(0, 4)
    def _(tile):
        cols = pl.ds(pl.multiple_of(tile * B, B), B)
        for a, src in enumerate((q_v, k_v, v_v)):
            ext[a, 8 : 8 + B, cols] = src[:, cols].astype(F32)
        for first_row in range(0, B, 32):
            gate(first_row, 32, tile)

    for load in loads[5:]:
        load.wait()
    tw_re, tw_im = twist[0], twist[1]

    def put_mid(block, stage):
        re, im = stage[:B], stage[B:]
        rows = pl.ds(pl.multiple_of(block * B, B), B)
        for half, value in ((0, re * tw_re - im * tw_im), (1, re * tw_im + im * tw_re)):
            high, low = split(value)
            mid_hi[rows, half * B : half * B + B] = high
            mid_lo[rows, half * B : half * B + B] = low

    def second_stage(chunk):
        rows = pl.ds(pl.multiple_of(chunk * 2 * B, 2 * B), 2 * B)
        high = mid_hi[rows, :]
        spec[rows, :] = dot(high, squares[1]) + dot(mid_lo[rows, :], squares[1]) + dot(high, squares[2])

    @pl.loop(0, PER // 2)
    def _(p):
        rows = [filt[pl.ds(2 * p + i, B, stride=PER), :] for i in range(2)]
        high, low = split(jnp.concatenate(rows, axis=1))
        first = squares[0]
        stage = dot(first, jnp.concatenate([high, high], axis=0)) + dot(first[:, :B], low)
        for i in range(2):
            put_mid(8 + 2 * p + i, stage[:, i * B : i * B + B])
        second_stage(4 + p)

    pl.semaphore_wait(barrier, n - 1)
    halo1 = halo_copy(halo_s, halo_r, dma_sems.at[0], dma_sems.at[1], 1)

    @pl.when(me < n - 1)
    def _():
        halo1.start()

    @pl.when(me > 0)
    def _():
        halo1.wait_recv()
        for a in range(3):
            ext[a, 0:8, :] = halo_r[a].astype(F32)

    @pl.loop(0, 4)
    def _(tile):
        gate(0, 16, tile)
        wide = pl.multiple_of(tile * 2 * B, 2 * B)
        rows = lax.dot_general(
            squares[6], pair[:, pl.ds(wide, 2 * B)], (((1,), (1,)), ((), ())),
            preferred_element_type=F32,
        )
        send1[pl.ds(pl.multiple_of(tile * 32, 32), 32)] = rows.reshape(32, 8, B).astype(BF16)

    exchange(send1, recv1, dma_sems.at[2], dma_sems.at[3])
    all1 = all_of(send1, recv1, dma_sems.at[2], dma_sems.at[3])
    all1.wait_recv()

    x32[...] = recv1[...].astype(F32).reshape(8 * B, B)

    @pl.loop(0, 4)
    def _(p):
        rows = [x32[pl.ds(2 * p + i, B, stride=8), :].astype(BF16) for i in range(2)]
        signal = jnp.concatenate(rows, axis=1)
        stage = dot(squares[0], jnp.concatenate([signal, signal], axis=0))
        for i in range(2):
            put_mid(2 * p + i, stage[:, i * B : i * B + B])
        second_stage(p)

    def put_prod(block, re, im):
        rows = pl.ds(pl.multiple_of(block * B, B), B)
        for half, value in ((0, re), (1, im)):
            high, low = split(value)
            prod_hi[rows, half * B : half * B + B] = high
            prod_lo[rows, half * B : half * B + B] = low

    def spectrum(block):
        rows = pl.ds(pl.multiple_of(block * B, B), B)
        return spec[rows, 0:B], spec[rows, B : 2 * B]

    @pl.loop(0, PER)
    def _(c):
        x_re, x_im = spectrum(c)
        h_re, h_im = spectrum(8 + c)
        put_prod(c, x_re * h_re - x_im * h_im, x_re * h_im + x_im * h_re)
        g_re, g_im = spectrum(4 + c)
        put_prod(4 + c, h_re * g_re + h_im * g_im, h_re * g_im - h_im * g_re)

    def back(chunk, scale):
        rows = pl.ds(pl.multiple_of(chunk * 2 * B, 2 * B), 2 * B)
        high = prod_hi[rows, :]
        mid = dot(high, squares[3]) + dot(prod_lo[rows, :], squares[3]) + dot(high, squares[4])
        mid = mid * scale
        sides = []
        for i in range(2):
            re, im = mid[i * B : i * B + B, :B], mid[i * B : i * B + B, B:]
            sides.append(
                jnp.concatenate([re * tw_re + im * tw_im, im * tw_re - re * tw_im], axis=0)
            )
        high, low = split(jnp.concatenate(sides, axis=1))
        both = dot(squares[5], high)
        return both[:B] + both[B:] + dot(squares[5, 0:B, :], low)

    @pl.loop(0, 4)
    def _(p):
        result = back(p, 1.0 / SEQ)
        for i in range(2):
            y32[pl.ds(2 * p + i, B, stride=8), :] = result[:, i * B : i * B + B]

    send2[...] = y32[...].reshape(B, 8, B).astype(BF16)
    exchange(send2, recv2, dma_sems.at[4], dma_sems.at[5])

    @pl.loop(0, PER)
    def _(c):
        x_re, x_im = spectrum(c)
        g_re, g_im = spectrum(4 + c)
        put_prod(8 + c, x_re * g_re + x_im * g_im, x_re * g_im - x_im * g_re)

    @pl.loop(0, PER // 2)
    def _(p):
        result = back(4 + p, 1.0 / (SEQ * math.sqrt(SEQ)))
        for i in range(2):
            fgrad_out[pl.ds(2 * p + i, B, stride=PER), :] = result[:, i * B : i * B + B]

    for a in range(3):
        ext_back[a, B : B + 8, :] = jnp.zeros((8, ext_back.shape[2]), F32)
    all2 = all_of(send2, recv2, dma_sems.at[4], dma_sems.at[5])
    all2.wait_recv()

    @pl.loop(0, 4)
    def _(tile):
        cols = pl.ds(pl.multiple_of(tile * B, B), B)
        arrived = recv2[pl.ds(pl.multiple_of(tile * 32, 32), 32)].astype(F32).reshape(2 * B, B)
        rows = dot(arrived.T.astype(BF16), squares[6])
        long, gated_back = rows[:, :B], rows[:, B:]
        mixed_out[:, cols] = (conv[0, :, cols] * long).astype(BF16)
        for a, value in (
            (0, g_v[:, cols].astype(F32) * long),
            (1, gated_back * conv[2, :, cols]),
            (2, gated_back * conv[1, :, cols]),
        ):
            rounded = value.astype(BF16)
            ext_back[a, 0:B, cols] = rounded.astype(F32)
            halo2_s[a, :, cols] = rounded[0:16][0:8]

    halo2 = halo_copy(halo2_s, halo2_r, dma_sems.at[6], dma_sems.at[7], -1)

    @pl.when(me > 0)
    def _():
        halo2.start()

    def reverse(a, first_row, rows, cols):
        acc = taps[a, 0:1, cols] * ext_back[a, first_row : first_row + rows, cols]
        for j in range(1, TAPS):
            start = first_row + j
            acc = acc + taps[a, j : j + 1, cols] * ext_back[a, start : start + rows, cols]
        grads_out[a, first_row : first_row + rows, cols] = acc.astype(BF16)

    @pl.loop(0, 4)
    def _(tile):
        cols = pl.ds(pl.multiple_of(tile * B, B), B)
        for a in range(3):
            for first_row, rows in ((0, 32), (32, 32), (64, 32), (96, 16)):
                reverse(a, first_row, rows, cols)

    @pl.when(me < n - 1)
    def _():
        halo2.wait_recv()
        for a in range(3):
            ext_back[a, B : B + 8, :] = halo2_r[a].astype(F32)

    @pl.loop(0, 4)
    def _(tile):
        cols = pl.ds(pl.multiple_of(tile * B, B), B)
        for a in range(3):
            reverse(a, B - 16, 16, cols)

    @pl.when(me < n - 1)
    def _():
        halo1.wait_send()

    @pl.when(me > 0)
    def _():
        halo2.wait_send()

    all1.wait_send()
    all2.wait_send()


def shards(query_proj, key_proj, value_proj, short_taps, long_filter, grad_mixed):
    rows, channels = query_proj.shape
    filt = long_filter.reshape(PER, B, B).transpose(1, 0, 2).reshape(PER * B, B)
    squares, twist = jnp.asarray(SQUARES), jnp.asarray(TWIST)
    operands = (query_proj, key_proj, value_proj, grad_mixed, short_taps, filt, squares, twist)
    tokens = pltpu.VMEM((rows, channels), BF16)
    edge = pltpu.VMEM((3, 8, channels), BF16)
    blocks = pltpu.VMEM((B, 8, B), BF16)
    tall = pltpu.VMEM((8 * B, B), F32)
    mid = pltpu.VMEM((12 * B, 2 * B), BF16)
    mixed, grads, fgrad = pl.pallas_call(
        kernel,
        name="hyena",
        out_shape=(
            jax.ShapeDtypeStruct((rows, channels), BF16),
            jax.ShapeDtypeStruct((3, rows, channels), BF16),
            jax.ShapeDtypeStruct((PER * B, B), F32),
        ),
        in_specs=[pl.BlockSpec(memory_space=pl.ANY)] * len(operands),
        out_specs=[pl.BlockSpec(memory_space=pltpu.VMEM)] * 3,
        scratch_shapes=[
            tokens, tokens, tokens, tokens,
            pltpu.VMEM(short_taps.shape, F32),
            pltpu.VMEM(filt.shape, F32),
            pltpu.VMEM(squares.shape, BF16),
            pltpu.VMEM(twist.shape, F32),
            pltpu.VMEM((3, rows + 8, channels), F32),
            pltpu.VMEM((3, rows + 8, channels), F32),
            pltpu.VMEM((3, rows, channels), F32),
            edge, edge, edge, edge,
            pltpu.VMEM((rows, 2 * channels), BF16),
            blocks, blocks, blocks, blocks,
            tall, tall,
            mid, mid,
            pltpu.VMEM((12 * B, 2 * B), F32),
            mid, mid,
            pltpu.SemaphoreType.DMA((len(operands),)),
            pltpu.SemaphoreType.DMA((8,)),
        ],
        compiler_params=pltpu.CompilerParams(collective_id=0, has_side_effects=True),
    )(*operands)
    filter_grad = fgrad.reshape(B, PER, B).transpose(1, 0, 2).reshape(1, PER, SEQ)
    return (mixed, grads, filter_grad)


def solution(mesh):
    return jax.shard_map(
        shards,
        mesh=mesh,
        in_specs=(
            P("context", "tensor"),
            P("context", "tensor"),
            P("context", "tensor"),
            P(None, None, "tensor"),
            P("tensor", "context", None),
            P("context", "tensor"),
        ),
        out_specs=(
            P("context", "tensor"),
            P(None, "context", "tensor"),
            P("tensor", "context", None),
        ),
        check_vma=False,
    )
```

profile of v0, /device:TPU:123, one launch (start us, length us, event | category | flops | bytes accessed | tf_op | source)
XLA Modules:
  0.0 65.9 jit_solution(9115225751136676861)
XLA Ops:
  0.6 61.2 %hyena.1 = (bf16[128,512]{1,0:T(8,128)(2,1)}, bf16[3,128,512]{2,1,0:T(8,128)(2,1)}, f32[512,128]{1,0:T(8,128)}) custom-call(bf16[128,512]{1,0:T(8,128)(2,1)} %q_in.1, bf16[128,512]{1,0:T(8,128)(2,1)} %k_in.1, bf16[128,512]{1,0:T(8,128)(2,1)} %v_in.1, bf16[128,512]{1,0:T(8,128)(2,1)} %g_in.1, f32[3,7,512]{2,1,0:T(8,128)} %taps_in.1, f32[512,128]{1,0:T(8,128)} %bitcast.10, ...), custom_call_target="tpu_custom_call" | custom-call | tf_op jit(solution)/shard_map/hyena/pallas_call | solution.py:348
  61.8 1.6 %copy.16 = bf16[128,512]{1,0:T(8,128)(2,1)} copy(bf16[128,512]{1,0:T(8,128)(2,1)} %get-tuple-element.12) | data formatting | bytes 262144
  63.4 0.0 copy-start
  63.4 1.8 %copy.17 = bf16[3,128,512]{2,1,0:T(8,128)(2,1)} copy(bf16[3,128,512]{2,1,0:T(8,128)(2,1)} %get-tuple-element.13) | data formatting | bytes 786432
  65.2 0.0 copy-done
  65.2 0.7 %copy.18 = f32[1,4,16384]{2,1,0:T(4,128)} copy(f32[1,4,16384]{2,1,0:T(4,128)S(1)} %bitcast.11) | data formatting | bytes 524288
Async XLA Ops:
  63.4 1.8 %copy-start = (f32[512,128]{1,0:T(8,128)S(1)}, f32[512,128]{1,0:T(8,128)}, u32[]{:S(2)}) copy-start(f32[512,128]{1,0:T(8,128)} %get-tuple-element.8) | copy-start | bytes 786436
where the time goes:
time: 66.1 us; the launch traced here: 65.9 us
  Pallas kernels  61.2 us (93%)
  local copies, waits for them, and re-layouts  4.08 us (6%)
    pallas_call x1, Pallas kernels, shards(): pl.pallas_call(kernel, name='hyena', out_shape=(jax.ShapeDtypeStruct((row...  61.2 us
    unnamed x5, local copies, waits for them, and re-layouts  4.08 us

commit v1 on v0

--- a/solution.py
+++ b/solution.py
@@ -15,6 +15,7 @@
 SEQ = B * B
 PER = 4
 TAPS = 7
+COLS = 16
 
 
 def split_np(table):
@@ -66,7 +67,7 @@
     ext, ext_back, conv, halo_s, halo_r, halo2_s, halo2_r,
     pair, send1, recv1, send2, recv2, x32, y32,
     mid_hi, mid_lo, spec, prod_hi, prod_lo,
-    in_sems, dma_sems,
+    in_sems, dma_sems, row_sem,
 ):
     me = lax.axis_index("context")
     n = B
@@ -84,12 +85,26 @@
         load.start()
 
     barrier = pltpu.get_barrier_semaphore()
-
-    @pl.loop(1, n)
+    row, col = me // COLS, lax.rem(me, COLS)
+
+    def signal(sem, peer):
+        pl.semaphore_signal(sem, inc=1, device_id={"context": peer}, device_id_type=MESH)
+
+    @pl.when(col == COLS - 1)
+    def _():
+        signal(barrier, lax.rem(me + 1, n))
+
+    @pl.when(col == 0)
+    def _():
+        signal(barrier, lax.rem(me + n - 1, n))
+
+    @pl.loop(1, n // COLS)
     def _(i):
-        pl.semaphore_signal(
-            barrier, inc=1, device_id={"context": lax.rem(me + i, n)}, device_id_type=MESH
-        )
+        signal(barrier, lax.rem(row + i, n // COLS) * COLS + col)
+
+    @pl.loop(1, COLS)
+    def _(i):
+        signal(barrier, row * COLS + lax.rem(col + i, COLS))
 
     def exchange(src, dst, send_sem, recv_sem):
         @pl.loop(1, n)
@@ -121,7 +136,28 @@
         ext[a, 0:8, :] = jnp.zeros((8, ext.shape[2]), F32)
         halo_s[a] = src[B - 16 : B, :][8:16]
 
-    loads[4].wait()
+    edge = jnp.logical_or(col == 0, col == COLS - 1)
+
+    @pl.when(edge)
+    def _():
+        pl.semaphore_wait(barrier, n // COLS + COLS - 1)
+
+    @pl.when(jnp.logical_not(edge))
+    def _():
+        pl.semaphore_wait(barrier, n // COLS + COLS - 2)
+
+    @pl.loop(1, COLS)
+    def _(i):
+        signal(row_sem, row * COLS + lax.rem(col + i, COLS))
+
+    halo1 = halo_copy(halo_s, halo_r, dma_sems.at[0], dma_sems.at[1], 1)
+
+    @pl.when(me < n - 1)
+    def _():
+        halo1.start()
+
+    for load in loads[4:]:
+        load.wait()
 
     def short(a, first_row, rows, cols):
         acc = taps[a, 0:1, cols] * ext[a, 8 + first_row : 8 + first_row + rows, cols]
@@ -150,8 +186,26 @@
         for first_row in range(0, B, 32):
             gate(first_row, 32, tile)
 
-    for load in loads[5:]:
-        load.wait()
+    @pl.when(me > 0)
+    def _():
+        halo1.wait_recv()
+        for a in range(3):
+            ext[a, 0:8, :] = halo_r[a].astype(F32)
+
+    @pl.loop(0, 4)
+    def _(tile):
+        gate(0, 16, tile)
+        wide = pl.multiple_of(tile * 2 * B, 2 * B)
+        rows = lax.dot_general(
+            squares[6], pair[:, pl.ds(wide, 2 * B)], (((1,), (1,)), ((), ())),
+            preferred_element_type=F32,
+        )
+        send1[pl.ds(pl.multiple_of(tile * 32, 32), 32)] = rows.reshape(32, 8, B).astype(BF16)
+
+    pl.semaphore_wait(row_sem, COLS - 1)
+    exchange(send1, recv1, dma_sems.at[2], dma_sems.at[3])
+    all1 = all_of(send1, recv1, dma_sems.at[2], dma_sems.at[3])
+
     tw_re, tw_im = twist[0], twist[1]
 
     def put_mid(block, stage):
@@ -177,36 +231,11 @@
             put_mid(8 + 2 * p + i, stage[:, i * B : i * B + B])
         second_stage(4 + p)
 
-    pl.semaphore_wait(barrier, n - 1)
-    halo1 = halo_copy(halo_s, halo_r, dma_sems.at[0], dma_sems.at[1], 1)
-
-    @pl.when(me < n - 1)
-    def _():
-        halo1.start()
-
-    @pl.when(me > 0)
-    def _():
-        halo1.wait_recv()
-        for a in range(3):
-            ext[a, 0:8, :] = halo_r[a].astype(F32)
-
-    @pl.loop(0, 4)
-    def _(tile):
-        gate(0, 16, tile)
-        wide = pl.multiple_of(tile * 2 * B, 2 * B)
-        rows = lax.dot_general(
-            squares[6], pair[:, pl.ds(wide, 2 * B)], (((1,), (1,)), ((), ())),
-            preferred_element_type=F32,
-        )
-        send1[pl.ds(pl.multiple_of(tile * 32, 32), 32)] = rows.reshape(32, 8, B).astype(BF16)
-
-    exchange(send1, recv1, dma_sems.at[2], dma_sems.at[3])
-    all1 = all_of(send1, recv1, dma_sems.at[2], dma_sems.at[3])
     all1.wait_recv()
 
     x32[...] = recv1[...].astype(F32).reshape(8 * B, B)
 
-    @pl.loop(0, 4)
+    @pl.loop(0, 4, unroll=4)
     def _(p):
         rows = [x32[pl.ds(2 * p + i, B, stride=8), :].astype(BF16) for i in range(2)]
         signal = jnp.concatenate(rows, axis=1)
@@ -226,7 +255,7 @@
         rows = pl.ds(pl.multiple_of(block * B, B), B)
         return spec[rows, 0:B], spec[rows, B : 2 * B]
 
-    @pl.loop(0, PER)
+    @pl.loop(0, PER, unroll=4)
     def _(c):
         x_re, x_im = spectrum(c)
         h_re, h_im = spectrum(8 + c)
@@ -249,7 +278,7 @@
         both = dot(squares[5], high)
         return both[:B] + both[B:] + dot(squares[5, 0:B, :], low)
 
-    @pl.loop(0, 4)
+    @pl.loop(0, 4, unroll=4)
     def _(p):
         result = back(p, 1.0 / SEQ)
         for i in range(2):
@@ -335,24 +364,39 @@
     all2.wait_send()
 
 
+def store(mixed_in, grads_in, fgrad_in, mixed_out, grads_out, fgrad_out, sems):
+    copies = [
+        pltpu.make_async_copy(src, dst, sems.at[i])
+        for i, (src, dst) in enumerate(
+            [(grads_in, grads_out), (fgrad_in, fgrad_out), (mixed_in, mixed_out)]
+        )
+    ]
+    for copy in copies:
+        copy.start()
+    for copy in copies:
+        copy.wait()
+
+
 def shards(query_proj, key_proj, value_proj, short_taps, long_filter, grad_mixed):
     rows, channels = query_proj.shape
     filt = long_filter.reshape(PER, B, B).transpose(1, 0, 2).reshape(PER * B, B)
     squares, twist = jnp.asarray(SQUARES), jnp.asarray(TWIST)
     operands = (query_proj, key_proj, value_proj, grad_mixed, short_taps, filt, squares, twist)
+    operands = tuple(pltpu.with_memory_space_constraint(x, pltpu.HBM) for x in operands)
     tokens = pltpu.VMEM((rows, channels), BF16)
     edge = pltpu.VMEM((3, 8, channels), BF16)
     blocks = pltpu.VMEM((B, 8, B), BF16)
     tall = pltpu.VMEM((8 * B, B), F32)
     mid = pltpu.VMEM((12 * B, 2 * B), BF16)
-    mixed, grads, fgrad = pl.pallas_call(
+    out_shape = (
+        jax.ShapeDtypeStruct((rows, channels), BF16),
+        jax.ShapeDtypeStruct((3, rows, channels), BF16),
+        jax.ShapeDtypeStruct((PER * B, B), F32),
+    )
+    results = pl.pallas_call(
         kernel,
         name="hyena",
-        out_shape=(
-            jax.ShapeDtypeStruct((rows, channels), BF16),
-            jax.ShapeDtypeStruct((3, rows, channels), BF16),
-            jax.ShapeDtypeStruct((PER * B, B), F32),
-        ),
+        out_shape=out_shape,
         in_specs=[pl.BlockSpec(memory_space=pl.ANY)] * len(operands),
         out_specs=[pl.BlockSpec(memory_space=pltpu.VMEM)] * 3,
         scratch_shapes=[
@@ -373,9 +417,19 @@
             mid, mid,
             pltpu.SemaphoreType.DMA((len(operands),)),
             pltpu.SemaphoreType.DMA((8,)),
+            pltpu.SemaphoreType.REGULAR,
         ],
-        compiler_params=pltpu.CompilerParams(collective_id=0, has_side_effects=True),
+        compiler_params=pltpu.CompilerParams(collective_id=0, has_side_effects=True, vmem_limit_bytes=24 * 1024 * 1024),
     )(*operands)
+    mixed, grads, fgrad = pl.pallas_call(
+        store,
+        name="store",
+        out_shape=out_shape,
+        in_specs=[pl.BlockSpec(memory_space=pltpu.VMEM)] * 3,
+        out_specs=[pl.BlockSpec(memory_space=pl.ANY)] * 3,
+        scratch_shapes=[pltpu.SemaphoreType.DMA((3,))],
+        compiler_params=pltpu.CompilerParams(vmem_limit_bytes=2 * 1024 * 1024),
+    )(*results)
     filter_grad = fgrad.reshape(B, PER, B).transpose(1, 0, 2).reshape(1, PER, SEQ)
     return (mixed, grads, filter_grad)
 

time: 66.1 us -> 57.1 us (0.86)
  Pallas kernels: 61.2 us -> 56.3 us
  local copies, waits for them, and re-layouts: 4.08 us -> 0 us
    pallas_call x1 -> x2, Pallas kernels: 61.2 us -> 56.3 us  [the longest x1 55.4 us: shards(): pl.pallas_call(kernel, name='hyena', out_shape=out_shape, in_specs=[pl.Bl...]
    unnamed x5 -> x0, local copies, waits for them, and re-layouts: 4.08 us -> none
where the time goes in v1:
time: 57.1 us; the launch traced here: 56.9 us
  Pallas kernels  56.3 us (99%)
  between operations  0.64 us (1%)
    pallas_call x1, Pallas kernels, shards(): pl.pallas_call(kernel, name='hyena', out_shape=out_shape, in_specs=[pl.Bl...  55.4 us

profile of v1, /device:TPU:123, one launch (start us, length us, event | category | flops | bytes accessed | tf_op | source)
XLA Modules:
  0.0 56.9 jit_solution(4644947702190989731)
XLA Ops:
  0.6 55.4 %hyena.1 = (bf16[128,512]{1,0:T(8,128)(2,1)S(1)}, bf16[3,128,512]{2,1,0:T(8,128)(2,1)S(1)}, f32[512,128]{1,0:T(8,128)S(1)}) custom-call(bf16[128,512]{1,0:T(8,128)(2,1)} %q_in.1, bf16[128,512]{1,0:T(8,128)(2,1)} %k_in.1, bf16[128,512]{1,0:T(8,128)(2,1)} %v_in.1, bf16[128,512]{1,0:T(8,128)(2,1)} %g_in.1, f32[3,7,512]{2,1,0:T(8,128)} %taps_in.1, ...), custom_call_target="tpu_custom_call" | custom-call | tf_op jit(solution)/shard_map/hyena/pallas_call | solution.py:396
  56.0 0.9 %store.1 = (bf16[128,512]{1,0:T(8,128)(2,1)}, bf16[3,128,512]{2,1,0:T(8,128)(2,1)}, f32[512,128]{1,0:T(8,128)}) custom-call(bf16[128,512]{1,0:T(8,128)(2,1)S(1)} %get-tuple-element.9.mixed_in, bf16[3,128,512]{2,1,0:T(8,128)(2,1)S(1)} %get-tuple-element.10.grads_in, f32[512,128]{1,0:T(8,128)S(1)} %get-tuple-element.11.fgrad_in), custom_call_target="tpu_custom_call" | custom-call | tf_op jit(solution)/shard_map/store/pallas_call | solution.py:424

commit v2 on v1

--- a/solution.py
+++ b/solution.py
@@ -44,7 +44,8 @@
     squares = np.stack(
         [first_cat, *split_np(second), *split_np(second_back), back_cat, perm.astype(jnp.bfloat16)]
     )
-    twist = np.stack([np.cos(phi), -np.sin(phi)]).astype(np.float32)
+    twist = np.stack([np.cos(phi), -np.sin(phi), np.cos(phi) / SEQ, np.sin(phi) / SEQ])
+    twist = twist.astype(np.float32)
     return squares, twist
 
 
@@ -106,16 +107,14 @@
     def _(i):
         signal(barrier, row * COLS + lax.rem(col + i, COLS))
 
-    def exchange(src, dst, send_sem, recv_sem):
-        @pl.loop(1, n)
-        def _(i):
-            peer = lax.rem(me + i, n)
+    def sender(src, dst, send_sem, recv_sem):
+        def send(peer):
             pltpu.make_async_remote_copy(
                 src_ref=src.at[peer], dst_ref=dst.at[me], send_sem=send_sem, recv_sem=recv_sem,
                 device_id={"context": peer}, device_id_type=MESH,
             ).start()
 
-        dst[pl.ds(me, 1)] = src[pl.ds(me, 1)]
+        return send
 
     def all_of(src, dst, send_sem, recv_sem):
         return pltpu.make_async_remote_copy(
@@ -202,11 +201,28 @@
         )
         send1[pl.ds(pl.multiple_of(tile * 32, 32), 32)] = rows.reshape(32, 8, B).astype(BF16)
 
+    send = sender(send1, recv1, dma_sems.at[2], dma_sems.at[3])
+    for i in range(1, n // COLS):
+        send(lax.rem(row + i, n // COLS) * COLS + col)
+
+    @pl.loop(0, (COLS - 1) // 3)
+    def _(i):
+        for u in range(3):
+            send(row * COLS + lax.rem(col + 3 * i + 1 + u, COLS))
+
     pl.semaphore_wait(row_sem, COLS - 1)
-    exchange(send1, recv1, dma_sems.at[2], dma_sems.at[3])
+
+    @pl.loop(1, n // COLS)
+    def _(i):
+        start = lax.rem(row + i, n // COLS) * COLS
+        for u in range(1, COLS):
+            send(start + lax.rem(col + u, COLS))
+
+    recv1[pl.ds(me, 1)] = send1[pl.ds(me, 1)]
     all1 = all_of(send1, recv1, dma_sems.at[2], dma_sems.at[3])
 
     tw_re, tw_im = twist[0], twist[1]
+    back_re, back_im = twist[2], twist[3]
 
     def put_mid(block, stage):
         re, im = stage[:B], stage[B:]
@@ -216,8 +232,7 @@
             mid_hi[rows, half * B : half * B + B] = high
             mid_lo[rows, half * B : half * B + B] = low
 
-    def second_stage(chunk):
-        rows = pl.ds(pl.multiple_of(chunk * 2 * B, 2 * B), 2 * B)
+    def second_stage(rows):
         high = mid_hi[rows, :]
         spec[rows, :] = dot(high, squares[1]) + dot(mid_lo[rows, :], squares[1]) + dot(high, squares[2])
 
@@ -229,7 +244,7 @@
         stage = dot(first, jnp.concatenate([high, high], axis=0)) + dot(first[:, :B], low)
         for i in range(2):
             put_mid(8 + 2 * p + i, stage[:, i * B : i * B + B])
-        second_stage(4 + p)
+        second_stage(pl.ds(pl.multiple_of((4 + p) * 2 * B, 2 * B), 2 * B))
 
     all1.wait_recv()
 
@@ -242,7 +257,8 @@
         stage = dot(squares[0], jnp.concatenate([signal, signal], axis=0))
         for i in range(2):
             put_mid(2 * p + i, stage[:, i * B : i * B + B])
-        second_stage(p)
+
+    second_stage(slice(0, 8 * B))
 
     def put_prod(block, re, im):
         rows = pl.ds(pl.multiple_of(block * B, B), B)
@@ -263,29 +279,37 @@
         g_re, g_im = spectrum(4 + c)
         put_prod(4 + c, h_re * g_re + h_im * g_im, h_re * g_im - h_im * g_re)
 
-    def back(chunk, scale):
-        rows = pl.ds(pl.multiple_of(chunk * 2 * B, 2 * B), 2 * B)
+    def second_back(rows):
         high = prod_hi[rows, :]
-        mid = dot(high, squares[3]) + dot(prod_lo[rows, :], squares[3]) + dot(high, squares[4])
-        mid = mid * scale
+        return dot(high, squares[3]) + dot(prod_lo[rows, :], squares[3]) + dot(high, squares[4])
+
+    def first_back(mid):
         sides = []
         for i in range(2):
             re, im = mid[i * B : i * B + B, :B], mid[i * B : i * B + B, B:]
             sides.append(
-                jnp.concatenate([re * tw_re + im * tw_im, im * tw_re - re * tw_im], axis=0)
+                jnp.concatenate([re * back_re - im * back_im, im * back_re + re * back_im], axis=0)
             )
         high, low = split(jnp.concatenate(sides, axis=1))
         both = dot(squares[5], high)
         return both[:B] + both[B:] + dot(squares[5, 0:B, :], low)
 
-    @pl.loop(0, 4, unroll=4)
-    def _(p):
-        result = back(p, 1.0 / SEQ)
+    mids = second_back(slice(0, 8 * B))
+    for p in range(4):
+        result = first_back(mids[2 * B * p : 2 * B * (p + 1)])
         for i in range(2):
             y32[pl.ds(2 * p + i, B, stride=8), :] = result[:, i * B : i * B + B]
 
     send2[...] = y32[...].reshape(B, 8, B).astype(BF16)
-    exchange(send2, recv2, dma_sems.at[4], dma_sems.at[5])
+    send = sender(send2, recv2, dma_sems.at[4], dma_sems.at[5])
+
+    @pl.loop(0, (n - 2) // 3)
+    def _(i):
+        for u in range(3):
+            send(lax.rem(me + 3 * i + 1 + u, n))
+
+    send(lax.rem(me + n - 1, n))
+    recv2[pl.ds(me, 1)] = send2[pl.ds(me, 1)]
 
     @pl.loop(0, PER)
     def _(c):
@@ -295,7 +319,8 @@
 
     @pl.loop(0, PER // 2)
     def _(p):
-        result = back(4 + p, 1.0 / (SEQ * math.sqrt(SEQ)))
+        mid = second_back(pl.ds(pl.multiple_of((4 + p) * 2 * B, 2 * B), 2 * B))
+        result = first_back(mid) * (1.0 / math.sqrt(SEQ))
         for i in range(2):
             fgrad_out[pl.ds(2 * p + i, B, stride=PER), :] = result[:, i * B : i * B + B]
 
@@ -304,27 +329,42 @@
     all2 = all_of(send2, recv2, dma_sems.at[4], dma_sems.at[5])
     all2.wait_recv()
 
-    @pl.loop(0, 4)
+    def gradients(here, cols, long, gated_back):
+        return (
+            (g_v[here, cols].astype(F32) * long).astype(BF16),
+            (gated_back * conv[2, here, cols]).astype(BF16),
+            (gated_back * conv[1, here, cols]).astype(BF16),
+        )
+
+    eye = jnp.where(
+        lax.broadcasted_iota(jnp.int32, (16, B), 0) == lax.broadcasted_iota(jnp.int32, (16, B), 1),
+        1.0, 0.0,
+    ).astype(BF16)
+    for tile in range(4):
+        cols = slice(tile * B, tile * B + B)
+        arrived = recv2[tile * 32 : tile * 32 + 32].astype(F32).reshape(2 * B, B).astype(BF16)
+        head = lax.dot_general(
+            eye, arrived, (((1,), (1,)), ((), ())), preferred_element_type=F32
+        ).astype(BF16)
+        head = dot(head, squares[6])
+        for a, value in enumerate(gradients(slice(0, 16), cols, head[:, :B], head[:, B:])):
+            halo2_s[a, :, cols] = value[0:8]
+
+    halo2 = halo_copy(halo2_s, halo2_r, dma_sems.at[6], dma_sems.at[7], -1)
+
+    @pl.when(me > 0)
+    def _():
+        halo2.start()
+
+    @pl.loop(0, 4, unroll=2)
     def _(tile):
         cols = pl.ds(pl.multiple_of(tile * B, B), B)
         arrived = recv2[pl.ds(pl.multiple_of(tile * 32, 32), 32)].astype(F32).reshape(2 * B, B)
         rows = dot(arrived.T.astype(BF16), squares[6])
         long, gated_back = rows[:, :B], rows[:, B:]
         mixed_out[:, cols] = (conv[0, :, cols] * long).astype(BF16)
-        for a, value in (
-            (0, g_v[:, cols].astype(F32) * long),
-            (1, gated_back * conv[2, :, cols]),
-            (2, gated_back * conv[1, :, cols]),
-        ):
-            rounded = value.astype(BF16)
-            ext_back[a, 0:B, cols] = rounded.astype(F32)
-            halo2_s[a, :, cols] = rounded[0:16][0:8]
-
-    halo2 = halo_copy(halo2_s, halo2_r, dma_sems.at[6], dma_sems.at[7], -1)
-
-    @pl.when(me > 0)
-    def _():
-        halo2.start()
+        for a, value in enumerate(gradients(slice(0, B), cols, long, gated_back)):
+            ext_back[a, 0:B, cols] = value.astype(F32)
 
     def reverse(a, first_row, rows, cols):
         acc = taps[a, 0:1, cols] * ext_back[a, first_row : first_row + rows, cols]
@@ -346,7 +386,7 @@
         for a in range(3):
             ext_back[a, B : B + 8, :] = halo2_r[a].astype(F32)
 
-    @pl.loop(0, 4)
+    @pl.loop(0, 4, unroll=True)
     def _(tile):
         cols = pl.ds(pl.multiple_of(tile * B, B), B)
         for a in range(3):

time: 57.1 us -> 55.6 us (0.974)
  the two profiles are of different devices: /device:TPU:123 before, /device:TPU:121 now
where the time goes in v2:
time: 55.6 us; the launch traced here: 55.5 us
  Pallas kernels  54.8 us (99%)
  between operations  0.64 us (1%)
    pallas_call x1, Pallas kernels, shards(): pl.pallas_call(kernel, name='hyena', out_shape=out_shape, in_specs=[pl.Bl...  53.9 us

profile of v2, /device:TPU:121, one launch (start us, length us, event | category | flops | bytes accessed | tf_op | source)
XLA Modules:
  0.0 55.5 jit_solution(8186438895512131741)
XLA Ops:
  0.6 53.9 %hyena.1 = (bf16[128,512]{1,0:T(8,128)(2,1)S(1)}, bf16[3,128,512]{2,1,0:T(8,128)(2,1)S(1)}, f32[512,128]{1,0:T(8,128)S(1)}) custom-call(bf16[128,512]{1,0:T(8,128)(2,1)} %q_in.1, bf16[128,512]{1,0:T(8,128)(2,1)} %k_in.1, bf16[128,512]{1,0:T(8,128)(2,1)} %v_in.1, bf16[128,512]{1,0:T(8,128)(2,1)} %g_in.1, f32[3,7,512]{2,1,0:T(8,128)} %taps_in.1, ...), custom_call_target="tpu_custom_call" | custom-call | tf_op jit(solution)/shard_map/hyena/pallas_call | solution.py:436
  54.6 0.9 %store.1 = (bf16[128,512]{1,0:T(8,128)(2,1)}, bf16[3,128,512]{2,1,0:T(8,128)(2,1)}, f32[512,128]{1,0:T(8,128)}) custom-call(bf16[128,512]{1,0:T(8,128)(2,1)S(1)} %get-tuple-element.9.mixed_in, bf16[3,128,512]{2,1,0:T(8,128)(2,1)S(1)} %get-tuple-element.10.grads_in, f32[512,128]{1,0:T(8,128)S(1)} %get-tuple-element.11.fgrad_in), custom_call_target="tpu_custom_call" | custom-call | tf_op jit(solution)/shard_map/store/pallas_call | solution.py:464

commit v3 on v2

--- a/solution.py
+++ b/solution.py
@@ -191,7 +191,7 @@
         for a in range(3):
             ext[a, 0:8, :] = halo_r[a].astype(F32)
 
-    @pl.loop(0, 4)
+    @pl.loop(0, 4, unroll=True)
     def _(tile):
         gate(0, 16, tile)
         wide = pl.multiple_of(tile * 2 * B, 2 * B)

time: 55.6 us -> 55 us (0.989)
  the two profiles are of different devices: /device:TPU:121 before, /device:TPU:89 now
where the time goes in v3:
time: 55 us; the launch traced here: 54.9 us
  Pallas kernels  54.2 us (99%)
  between operations  0.64 us (1%)
    pallas_call x1, Pallas kernels, shards(): pl.pallas_call(kernel, name='hyena', out_shape=out_shape, in_specs=[pl.Bl...  53.3 us

profile of v3, /device:TPU:89, one launch (start us, length us, event | category | flops | bytes accessed | tf_op | source)
XLA Modules:
  0.0 54.9 jit_solution(4267297573140219162)
XLA Ops:
  0.6 53.3 %hyena.1 = (bf16[128,512]{1,0:T(8,128)(2,1)S(1)}, bf16[3,128,512]{2,1,0:T(8,128)(2,1)S(1)}, f32[512,128]{1,0:T(8,128)S(1)}) custom-call(bf16[128,512]{1,0:T(8,128)(2,1)} %q_in.1, bf16[128,512]{1,0:T(8,128)(2,1)} %k_in.1, bf16[128,512]{1,0:T(8,128)(2,1)} %v_in.1, bf16[128,512]{1,0:T(8,128)(2,1)} %g_in.1, f32[3,7,512]{2,1,0:T(8,128)} %taps_in.1, ...), custom_call_target="tpu_custom_call" | custom-call | tf_op jit(solution)/shard_map/hyena/pallas_call | solution.py:436
  54.0 0.9 %store.1 = (bf16[128,512]{1,0:T(8,128)(2,1)}, bf16[3,128,512]{2,1,0:T(8,128)(2,1)}, f32[512,128]{1,0:T(8,128)}) custom-call(bf16[128,512]{1,0:T(8,128)(2,1)S(1)} %get-tuple-element.9.mixed_in, bf16[3,128,512]{2,1,0:T(8,128)(2,1)S(1)} %get-tuple-element.10.grads_in, f32[512,128]{1,0:T(8,128)S(1)} %get-tuple-element.11.fgrad_in), custom_call_target="tpu_custom_call" | custom-call | tf_op jit(solution)/shard_map/store/pallas_call | solution.py:464
